TPU v7x, 128 devices: a whole 4x4x4 slice. The times are simulated.
128 devices in a mesh: row: 8 (over z, core), col: 16 (over y, x).
Axes of the slice: x: 4, y: 4, z: 4, core: 2. Of those that a mesh axis runs over, the one named last changes fastest.
Arguments:
- hidden: bfloat16 [1408, 16384], P('col', 'row'), may hold values from -18 to 18
- gain_in: bfloat16 [1408], replicated, may hold values from 0.5 to 1.5
- w_query: bfloat16 [1408, 1408], P('col'), may hold values from -0.3125 to 0.3125
- w_pair: bfloat16 [2, 1408, 1408], P(None, 'col'), may hold values from -0.15625 to 0.15625
- kv_cache: bfloat16 [2, 1408, 16384], P(None, 'col', 'row'), may hold values from -103 to 103
- recompute_rows: int32 [8, 200], P('row'), may hold values from 0 to 2047, as said below
- segment_ids: int32 [16384], P('row'), may hold values from -1 to 1, as said below
- w_out: bfloat16 [1408, 1408], P('col'), may hold values from -0.3125 to 0.3125
- gain_merge: bfloat16 [1408], replicated, may hold values from 0.5 to 1.5
- w_merge: bfloat16 [4, 1408, 1408], P(None, 'col'), may hold values from -0.078125 to 0.078125
- requests: int32 [8, 16, 85], P('row'), may hold values from -1 to 511, as said below
Outputs:
- delivered: bfloat16 [8, 16, 85, 1408], P('row', 'col')
Inputs may be any that keep to these rules, and one draw needn't show every extreme that they name: `segment_ids`: ids do not fall along the tokens except to -1 for the padding at the end; every image covers a multiple of 4 tokens and starts at a multiple of 4. `recompute_rows`: the 200 offsets of one index of row are distinct. `requests`: for each index of row, the lists of all owners together name each of its 512 merged tokens exactly once; unused slots hold -1 and follow the used ones.
All inputs are finite; a program needn't handle non-finite values.
Results may differ from a plain program's by a relative error of at most 0.025.
The roundings to bfloat16 on the way count: a program that leaves them out, or rounds other values in their place, can miss the bound.
Values may be sent and summed in bfloat16 or wider, within the bound.
A program may use at most 128 MiB of HBM per device.

v0:
```python
import jax
import jax.numpy as jnp
from jax import lax
import functools
from jax.experimental import pallas as pl
from jax.experimental.pallas import tpu as pltpu
from jax.sharding import PartitionSpec as P

HD = 88


EPSILON = 1e-06
MASKED = -1e30
PADW = 96
Q_BLOCK = 2048
K_BLOCK = 2048


def _attn_kernel(kb_map, flags, q_ref, qs_ref, k_ref, v_ref, o_ref, m_ref, l_ref, acc_ref, *, scale, n_steps):
    qb = pl.program_id(0)
    j = pl.program_id(1)
    flag = flags[qb, j]

    @pl.when(j == 0)
    def _():
        m_ref[...] = jnp.full(m_ref.shape, MASKED, jnp.float32)
        l_ref[...] = jnp.zeros(l_ref.shape, jnp.float32)
        acc_ref[...] = jnp.zeros(acc_ref.shape, jnp.float32)

    def step(masked):
        q = q_ref[...]
        k = k_ref[...]
        s = jnp.dot(q, k, preferred_element_type=jnp.float32) * scale
        if masked:
            key_seg = k[HD:HD + 1, :].astype(jnp.float32)
            s = jnp.where(qs_ref[...] == key_seg, s, MASKED)
        m_prev = m_ref[...]
        m_new = jnp.maximum(m_prev, jnp.max(s, axis=1, keepdims=True))
        p = jnp.exp(s - m_new)
        alpha = jnp.exp(m_prev - m_new)
        l_ref[...] = alpha * l_ref[...] + jnp.sum(p, axis=1, keepdims=True)
        pv = lax.dot_general(
            p.astype(jnp.bfloat16), v_ref[...], (((1,), (1,)), ((), ())),
            preferred_element_type=jnp.float32,
        )
        acc_ref[...] = alpha * acc_ref[...] + pv
        m_ref[...] = m_new

    @pl.when(flag == 1)
    def _():
        step(True)

    @pl.when(flag == 2)
    def _():
        step(False)

    @pl.when(j == n_steps - 1)
    def _():
        o_ref[...] = (acc_ref[...] / l_ref[...]).astype(o_ref.dtype)


def _row_gather_kernel(x_ref, o_ref, send_far, recv_far, send_pair, recv_pair, send_fwd, recv_fwd, local_sem, *, n_row):
    mesh_ids = pl.DeviceIdType.MESH
    n_chip = n_row // 2
    me = lax.axis_index("row")
    col = lax.axis_index("col")
    chip = me // 2
    core = me % 2
    sibling = chip * 2 + 1 - core
    far = [lax.rem(chip + k, n_chip) * 2 + core for k in range(1, n_chip)]
    barrier = pltpu.get_barrier_semaphore()
    for peer in far + [sibling]:
        pl.semaphore_signal(barrier, inc=1, device_id=(peer, col), device_id_type=mesh_ids)
    pl.semaphore_wait(barrier, n_chip)
    local = pltpu.make_async_copy(x_ref, o_ref.at[me], local_sem)
    local.start()
    pair = pltpu.make_async_remote_copy(
        src_ref=x_ref, dst_ref=o_ref.at[me], send_sem=send_pair, recv_sem=recv_pair,
        device_id=(sibling, col), device_id_type=mesh_ids,
    )
    pair.start()
    outgoing = []
    for k in range(1, n_chip):
        copy = pltpu.make_async_remote_copy(
            src_ref=x_ref, dst_ref=o_ref.at[me], send_sem=send_far.at[k], recv_sem=recv_far.at[k],
            device_id=(far[k - 1], col), device_id_type=mesh_ids,
        )
        copy.start()
        outgoing.append(copy)
    forwards = []
    for k in range(1, n_chip):
        outgoing[k - 1].wait_recv()
        source = lax.rem(chip + n_chip - k, n_chip) * 2 + core
        forward = pltpu.make_async_remote_copy(
            src_ref=o_ref.at[source], dst_ref=o_ref.at[source], send_sem=send_fwd.at[k],
            recv_sem=recv_fwd.at[k], device_id=(sibling, col), device_id_type=mesh_ids,
        )
        forward.start()
        forwards.append(forward)
    local.wait()
    pair.wait()
    for copy in outgoing:
        copy.wait_send()
    for forward in forwards:
        forward.wait()


def row_gather(x, n_row):
    n_chip = n_row // 2
    return pl.pallas_call(
        functools.partial(_row_gather_kernel, n_row=n_row),
        out_shape=jax.ShapeDtypeStruct((n_row,) + x.shape, x.dtype),
        in_specs=[pl.BlockSpec(memory_space=pl.ANY)],
        out_specs=pl.BlockSpec(memory_space=pl.ANY),
        scratch_shapes=[
            pltpu.SemaphoreType.DMA((n_chip,)),
            pltpu.SemaphoreType.DMA((n_chip,)),
            pltpu.SemaphoreType.DMA,
            pltpu.SemaphoreType.DMA,
            pltpu.SemaphoreType.DMA((n_chip,)),
            pltpu.SemaphoreType.DMA((n_chip,)),
            pltpu.SemaphoreType.DMA,
        ],
        compiler_params=pltpu.CompilerParams(collective_id=0, has_side_effects=True),
    )(x)


def _col_gather_kernel(x_ref, o_ref, send_sems, recv_sems, local_sem, *, n_col):
    mesh_ids = pl.DeviceIdType.MESH
    me = lax.axis_index("col")
    row = lax.axis_index("row")
    barrier = pltpu.get_barrier_semaphore()
    for k in range(1, n_col):
        peer = lax.rem(me + k, n_col)
        pl.semaphore_signal(barrier, inc=1, device_id=(row, peer), device_id_type=mesh_ids)
    pl.semaphore_wait(barrier, n_col - 1)
    local = pltpu.make_async_copy(x_ref, o_ref.at[me], local_sem)
    local.start()
    copies = []
    for k in range(1, n_col):
        peer = lax.rem(me + k, n_col)
        copy = pltpu.make_async_remote_copy(
            src_ref=x_ref, dst_ref=o_ref.at[me], send_sem=send_sems.at[k], recv_sem=recv_sems.at[k],
            device_id=(row, peer), device_id_type=mesh_ids,
        )
        copy.start()
        copies.append(copy)
    local.wait()
    for copy in copies:
        copy.wait()


def col_gather(x, n_col):
    return pl.pallas_call(
        functools.partial(_col_gather_kernel, n_col=n_col),
        out_shape=jax.ShapeDtypeStruct((n_col,) + x.shape, x.dtype),
        in_specs=[pl.BlockSpec(memory_space=pl.ANY)],
        out_specs=pl.BlockSpec(memory_space=pl.ANY),
        scratch_shapes=[
            pltpu.SemaphoreType.DMA((n_col,)),
            pltpu.SemaphoreType.DMA((n_col,)),
            pltpu.SemaphoreType.DMA,
        ],
        compiler_params=pltpu.CompilerParams(collective_id=1, has_side_effects=True),
    )(x)


def block_tables(q_seg, k_seg, q_start):
    n_q = q_seg.shape[0] // Q_BLOCK
    n_k = k_seg.shape[0] // K_BLOCK
    values = jnp.arange(-1, 2, dtype=jnp.int32)
    q_has = jnp.any(q_seg.reshape(n_q, Q_BLOCK, 1) == values, axis=1).astype(jnp.float32)
    k_has = jnp.any(k_seg.reshape(n_k, K_BLOCK, 1) == values, axis=1).astype(jnp.float32)
    shared = jnp.dot(q_has, k_has.T) > 0
    single = (jnp.sum(q_has, axis=1)[:, None] == 1) & (jnp.sum(k_has, axis=1)[None, :] == 1)
    diag = (q_start + jnp.arange(n_q, dtype=jnp.int32) * Q_BLOCK) // K_BLOCK
    order = (diag[:, None] + jnp.arange(n_k, dtype=jnp.int32)[None, :]) % n_k
    need = jnp.take_along_axis(shared, order, axis=1)
    full = jnp.take_along_axis(single, order, axis=1)
    rank = jnp.cumsum(need.astype(jnp.int32), axis=1) - 1
    count = jnp.sum(need.astype(jnp.int32), axis=1)
    pos = jnp.where(need, rank, n_k + jnp.arange(n_k)[None, :])
    perm = jnp.argsort(pos, axis=1)
    kb_sorted = jnp.take_along_axis(order, perm, axis=1)
    full_sorted = jnp.take_along_axis(full, perm, axis=1)
    step = jnp.arange(n_k, dtype=jnp.int32)[None, :]
    live = step < count[:, None]
    last = jnp.take_along_axis(kb_sorted, (count - 1)[:, None], axis=1)
    kb_map = jnp.where(live, kb_sorted, last).astype(jnp.int32)
    flags = jnp.where(live, jnp.where(full_sorted, 2, 1), 0).astype(jnp.int32)
    return kb_map, flags


def attention(q_t, q_seg_f, kv, kb_map, flags, scale, interpret=False):
    n_tok = q_t.shape[0]
    per_peer = kv.shape[3] // K_BLOCK
    n_keys = kv.shape[0] * kv.shape[3]
    n_q = n_tok // Q_BLOCK
    n_k = n_keys // K_BLOCK
    kernel = functools.partial(_attn_kernel, scale=scale, n_steps=n_k)
    grid_spec = pltpu.PrefetchScalarGridSpec(
        num_scalar_prefetch=2,
        grid=(n_q, n_k),
        in_specs=[
            pl.BlockSpec((Q_BLOCK, PADW), lambda i, j, km, fl: (i, 0)),
            pl.BlockSpec((Q_BLOCK, 1), lambda i, j, km, fl: (i, 0)),
            pl.BlockSpec((None, None, PADW, K_BLOCK), lambda i, j, km, fl: (km[i, j] // per_peer, 0, 0, km[i, j] % per_peer)),
            pl.BlockSpec((None, None, PADW, K_BLOCK), lambda i, j, km, fl: (km[i, j] // per_peer, 1, 0, km[i, j] % per_peer)),
        ],
        out_specs=pl.BlockSpec((Q_BLOCK, PADW), lambda i, j, km, fl: (i, 0)),
        scratch_shapes=[
            pltpu.VMEM((Q_BLOCK, 1), jnp.float32),
            pltpu.VMEM((Q_BLOCK, 1), jnp.float32),
            pltpu.VMEM((Q_BLOCK, PADW), jnp.float32),
        ],
    )
    return pl.pallas_call(
        kernel,
        grid_spec=grid_spec,
        out_shape=jax.ShapeDtypeStruct((n_tok, PADW), jnp.bfloat16),
        compiler_params=pltpu.CompilerParams(dimension_semantics=("arbitrary", "arbitrary")),
        interpret=interpret,
    )(kb_map, flags, q_t, q_seg_f, kv, kv)


def on_device(
    n_row,
    hidden,
    gain_in,
    w_query,
    w_pair,
    kv_cache,
    recompute_rows,
    segment_ids,
    w_out,
    gain_merge,
    w_merge,
    requests,
):
    local_width, tok_rows = hidden.shape
    model_width = w_query.shape[1]
    n_col = model_width // local_width
    heads_here = local_width // HD
    score_scale = HD ** (-0.5)
    col_index = lax.axis_index("col")
    gathered_rows = lax.all_gather(hidden, "col", axis=0, tiled=True)
    picked_rows = recompute_rows[0]
    hidden_picked = jnp.take(hidden, picked_rows, axis=1)
    picked_copies = jnp.broadcast_to(hidden_picked[None], (n_col,) + hidden_picked.shape)
    picked_full = lax.all_to_all(picked_copies, "col", 0, 0, tiled=True)
    picked_float = picked_full.reshape(model_width, -1).astype(jnp.float32)
    picked_mean = jnp.sum(picked_float, axis=0, keepdims=True) / model_width
    picked_square = jnp.sum(picked_float * picked_float, axis=0, keepdims=True) / model_width
    normed_picked = (
        (picked_float - picked_mean)
        * lax.rsqrt(picked_square - picked_mean * picked_mean + EPSILON)
        * gain_in.astype(jnp.float32)[:, None]
    ).astype(jnp.bfloat16)
    fresh_pairs = jnp.dot(
        w_pair.reshape(2 * local_width, model_width),
        normed_picked,
        preferred_element_type=jnp.float32,
    )
    fresh_pairs = fresh_pairs.astype(jnp.bfloat16).reshape(2, local_width, -1)
    keys_values = kv_cache.at[:, :, picked_rows].set(fresh_pairs)

    pair_local = jnp.pad(keys_values, ((0, 0), (0, PADW - HD), (0, 0)))
    pair_local = pair_local.at[0, HD].set(segment_ids.astype(jnp.bfloat16))
    pair_all = row_gather(pair_local, n_row)
    full_rows, pair_all = lax.optimization_barrier((gathered_rows, pair_all))
    full_float = full_rows.astype(jnp.float32)
    in_mean = jnp.sum(full_float, axis=0, keepdims=True) / model_width
    in_square = jnp.sum(full_float * full_float, axis=0, keepdims=True) / model_width
    normed = (
        (full_float - in_mean)
        * lax.rsqrt(in_square - in_mean * in_mean + EPSILON)
        * gain_in.astype(jnp.float32)[:, None]
    ).astype(jnp.bfloat16)
    query_rows = lax.dot_general(
        normed, w_query, (((0,), (1,)), ((), ())), preferred_element_type=jnp.float32
    ).astype(jnp.bfloat16)
    query_rows = jnp.pad(query_rows, ((0, 0), (0, PADW - HD)))
    segment_line = pair_all[:, 0, HD].reshape(-1).astype(jnp.int32)
    half = -(-model_width // 256) * 128
    core = lax.axis_index("row") % 2
    weight_stack = jnp.concatenate([w_out[None], w_merge], axis=0)
    weight_stack = jnp.pad(weight_stack, ((0, 0), (0, 0), (0, 2 * half - model_width)))
    weight_half = lax.dynamic_slice_in_dim(weight_stack, core * half, half, 2)
    weight_half, _ = lax.optimization_barrier((weight_half, picked_full))
    weights_mine = lax.all_gather(weight_half, "col", axis=1, tiled=True)

    def in_order(mine, other, axis):
        return jnp.where(
            core == 0,
            jnp.concatenate([mine, other], axis=axis),
            jnp.concatenate([other, mine], axis=axis),
        )
    kb_map, flags = block_tables(segment_ids, segment_line, lax.axis_index("row") * tok_rows)
    attended_rows = attention(
        query_rows, segment_ids.astype(jnp.float32)[:, None], pair_all, kb_map, flags, score_scale
    )
    attended = attended_rows[:, :HD].T
    weights_mine, _ = lax.optimization_barrier((weights_mine, attended_rows))
    weights_other = lax.ppermute(weights_mine, "row", [(i, i ^ 1) for i in range(n_row)])
    chunk = tok_rows // n_col
    attended_chunk = lax.all_to_all(attended, "col", 1, 0, tiled=True)
    x_chunk = lax.dynamic_slice_in_dim(full_rows, col_index * chunk, chunk, 1).astype(jnp.float32)
    projected = in_order(
        *[
            lax.dot_general(
                part[0], attended_chunk, (((0,), (0,)), ((), ())), preferred_element_type=jnp.float32
            )
            for part in (weights_mine, weights_other)
        ],
        0,
    )[:model_width]
    updated = x_chunk + projected
    row_mean = jnp.sum(updated, axis=0, keepdims=True) / model_width
    row_square = jnp.sum(updated * updated, axis=0, keepdims=True) / model_width
    merger_chunk = (
        (updated - row_mean)
        * lax.rsqrt(row_square - row_mean * row_mean + EPSILON)
        * gain_merge.astype(jnp.float32)[:, None]
    ).astype(jnp.bfloat16)
    grouped = merger_chunk.reshape(model_width, chunk // 4, 4)
    merged_here = in_order(
        *[
            jnp.einsum("fgi,ifd->gd", grouped, part[1:], preferred_element_type=jnp.float32)
            for part in (weights_mine, weights_other)
        ],
        1,
    )[:, :model_width]
    merged_all = col_gather(merged_here.astype(jnp.bfloat16), n_col).reshape(-1, model_width)
    wanted_rows = lax.dynamic_index_in_dim(requests[0], col_index, 0, keepdims=False)
    is_valid = wanted_rows >= 0
    safe_index = jnp.where(is_valid, wanted_rows, 0)
    picked = jnp.where(is_valid[:, None], merged_all[safe_index], jnp.zeros((), jnp.bfloat16))
    return picked.reshape(1, 1, picked.shape[0], model_width)


def solution(mesh):
    placed = (
        P("col", "row"),
        P(),
        P("col", None),
        P(None, "col", None),
        P(None, "col", "row"),
        P("row", None),
        P("row"),
        P("col", None),
        P(),
        P(None, "col", None),
        P("row", None, None),
    )
    return jax.shard_map(
        functools.partial(on_device, mesh.shape["row"]),
        mesh=mesh,
        in_specs=placed,
        out_specs=P("row", "col", None, None),
        check_vma=False,
    )
```

profile of v0, /device:TPU:78, one launch (start us, length us, event | category | flops | bytes accessed | tf_op | source)
XLA Modules:
  0.0 242.4 jit_solution(4779461130579702484)
XLA Ops:
  6.6 0.7 all-gather.3.cloned.1.call-update
  7.3 1.3 copy.56
  8.5 0.7 compare_select_fusion
  9.2 0.8 gather_fusion
  10.0 0.7 compare_and_fusion.3
  10.9 0.9 broadcast_in_dim.54
  11.8 7.3 %all-to-all-start = ((bf16[16,88,200]{2,1,0:T(8,128)(2,1)}), bf16[16,88,200]{2,1,0:T(8,128)(2,1)S(1)}, u32[]{:S(2)}, u32[]{:S(2)}) async-start(bf16[16,88,200]{2,1,0:T(8,128)(2,1)} %broadcast_in_dim.54), calls=%async_computation | async-start | bytes 1441792 | tf_op jit(solution)/shard_map/all_to_all | solution.py:250
  19.2 2.2 fusion.32
  21.4 10.6 %all-to-all-done = bf16[16,88,200]{2,1,0:T(8,128)(2,1)S(1)} async-done(((bf16[16,88,200]{2,1,0:T(8,128)(2,1)}), bf16[16,88,200]{2,1,0:T(8,128)(2,1)S(1)}, u32[]{:S(2)}, u32[]{:S(2)}) %all-to-all-start) | async-done | bytes 563232 | tf_op jit(solution)/shard_map/all_to_all | solution.py:250
  32.1 0.8 copy.59
  32.9 1.4 copy.69.qs_ref
  35.8 0.7 fusion.48
  36.5 0.7 and_reduce_fusion
  38.2 6.9 %scatter_fusion = bf16[2,88,2048]{1,0,2:T(2,128)(2,1)S(1)} fusion(bf16[2,88,2048]{1,0,2:T(2,128)(2,1)S(1)} %copy.59, s32[200]{0:T(256)S(1)} %bitcast.109, bf16[200,2,88]{2,1,0:T(2,128)(2,1)S(1)} %bitcast.101), kind=kCustom, calls=%fused_computation.6 | custom fusion | bytes 212000 | tf_op jit(solution)/shard_map/scatter | solution.py:265
  45.1 0.8 copy.60
  45.9 1.9 broadcast_select_fusion
  47.9 1.4 scatter.13.x_ref
  49.3 0.9 copy-done.2
  50.2 39.9 %shard_map.109.k_ref.v_ref = bf16[8,2,96,2048]{3,2,1,0:T(8,128)(2,1)} custom-call(bf16[2,96,2048]{2,1,0:T(8,128)(2,1)} %copy-done.2), custom_call_target="tpu_custom_call" | custom-call | tf_op jit(solution)/shard_map/pallas_call | solution.py:110
  90.1 4.4 %convert_reduce_fusion = (f32[2048]{0:T(1024)S(1)}, f32[2048]{0:T(1024)S(1)}) fusion(bf16[1408,2048]{1,0:T(8,128)(2,1)} %all-gather.3.cloned.1.call-done), kind=kLoop, calls=%fused_computation.9 | loop fusion | flops 11530240 | bytes 5783552 | tf_op jit(solution)/shard_map/reduce_sum | solution.py:272
  94.6 2.0 fusion.10
  96.9 0.9 pad.17.q_ref
  97.8 1.0 slice_convert_fusion
  99.2 0.7 gather_fusion.3
  100.1 0.7 convert_reduce_fusion.4
  101.6 0.7 sort.17
  103.0 0.6 gather_fusion.1
  103.7 0.6 gather_fusion.5
  104.3 1.2 compare_select_fusion.8
  105.5 0.6 fusion.49
  106.2 1.8 compare_select_fusion.9.kb_map
  108.0 53.0 %shard_map.110 = bf16[2048,96]{1,0:T(8,128)(2,1)} custom-call(s32[1,8]{1,0:T(1,128)} %compare_select_fusion.9.kb_map, s32[1,8]{1,0:T(1,128)} %get-tuple-element.53.flags, bf16[2048,96]{1,0:T(8,128)(2,1)} %pad.17.q_ref, f32[2048,1]{1,0:T(8,128)} %copy.69.qs_ref, bf16[8,2,96,2048]{3,2,1,0:T(8,128)(2,1)} %shard_map.109.k_ref.v_ref, ...), custom_call_target="tpu_custom_call" | custom-call | tf_op jit(solution)/shard_map/pallas_call | solution.py:217
  161.0 11.1 %collective-permute-start = (bf16[5,1408,768]{2,1,0:T(8,128)(2,1)}, bf16[5,1408,768]{2,1,0:T(8,128)(2,1)}, u32[]{:S(2)}, u32[]{:S(2)}) collective-permute-start(bf16[5,1408,768]{2,1,0:T(8,128)(2,1)} %all-gather.5.cloned.1.call-done), channel_id=1, source_target_pairs={{0,16},{16,0},{32,48},{48,32},{64,80},{80,64},{96,112},{112,96},{1... | collective-permute-start | bytes 32440328 | tf_op jit(solution)/shard_map/ppermute | solution.py:304
  172.1 2.0 copy.70
  174.1 9.5 %all-to-all-start.1 = ((bf16[88,16,128]{2,0,1:T(8,128)(2,1)}), bf16[88,16,128]{2,0,1:T(8,128)(2,1)S(1)}, u32[]{:S(2)}, u32[]{:S(2)}) async-start(bf16[88,16,128]{2,0,1:T(8,128)(2,1)} %copy.70), calls=%async_computation.1 | async-start | bytes 720896 | tf_op jit(solution)/shard_map/all_to_all | solution.py:306
  183.6 0.7 fusion.41
  184.3 0.7 compare_bitcast_fusion
  185.0 5.0 %all-to-all-done.1 = bf16[88,16,128]{2,0,1:T(8,128)(2,1)S(1)} async-done(((bf16[88,16,128]{2,0,1:T(8,128)(2,1)}), bf16[88,16,128]{2,0,1:T(8,128)(2,1)S(1)}, u32[]{:S(2)}, u32[]{:S(2)}) %all-to-all-start.1) | async-done | bytes 360480 | tf_op jit(solution)/shard_map/all_to_all | solution.py:306
  190.0 2.4 fusion.14
  192.4 2.4 fusion.13
  194.8 1.2 fusion.46
  196.0 1.2 multiply_convert_fusion
  197.6 5.0 %fusion.23 = bf16[32,768]{1,0:T(8,128)(2,1)S(1)} fusion(bf16[5,1408,768]{2,1,0:T(8,128)(2,1)} %all-gather.5.cloned.1.call-done, bf16[1408,32,4]{0,2,1:T(4,128)(2,1)S(1)} %reshape.459), kind=kOutput, calls=%fused_computation.38 | convolution fusion | flops 276824064 | bytes 9060352 | tf_op jit(solution)/shard_map/fgi,ifd->gd/dot_general | solution.py:328
  202.5 5.0 %fusion.26 = bf16[32,768]{1,0:T(8,128)(2,1)S(1)} fusion(bf16[5,1408,768]{2,1,0:T(8,128)(2,1)} %collective-permute-done, bf16[1408,32,4]{0,2,1:T(4,128)(2,1)S(1)} %reshape.459), kind=kOutput, calls=%fused_computation.39 | convolution fusion | flops 276824064 | bytes 9060352 | tf_op jit(solution)/shard_map/fgi,ifd->gd/dot_general | solution.py:328
  207.5 0.7 fusion.36.x_ref
  208.2 24.0 %shard_map.111 = bf16[16,32,1408]{2,1,0:T(8,128)(2,1)} custom-call(bf16[32,1408]{1,0:T(8,128)(2,1)} %fusion.36.x_ref), custom_call_target="tpu_custom_call" | custom-call | tf_op jit(solution)/shard_map/pallas_call | solution.py:154
  232.2 2.5 %gather_fusion.2 = bf16[85,1408]{1,0:T(8,128)(2,1)S(1)} fusion(bf16[512,1408]{1,0:T(8,128)(2,1)} %bitcast.98, s32[1024]{0:T(1024)S(1)} %pad_clamp_fusion), kind=kCustom, calls=%fused_computation.5 | custom fusion | bytes 479060 | tf_op jit(solution)/shard_map/gather | solution.py:337
  234.8 0.8 bitcast_select_fusion
  (62 shorter events, 4.4 us)
Async XLA Ops:
  6.5 31.2 %copy-start = (bf16[2,88,1408]{2,1,0:T(8,128)(2,1)S(1)}, bf16[2,88,1408]{2,1,0:T(8,128)(2,1)}, u32[]{:S(2)}) copy-start(bf16[2,88,1408]{2,1,0:T(8,128)(2,1)} %param.18) | copy-start | bytes 1486852
  6.5 29.9 %copy-start.7 = (s32[3]{0:T(128)S(1)}, s32[3]{0:T(128)}, u32[]{:S(2)}) copy-start(s32[3]{0:T(128)} %constant.172.clone.1) | copy-start | bytes 40
  6.5 25.5 %copy-start.5 = (bf16[1408]{0:T(1024)(128)(2,1)S(1)}, bf16[1408]{0:T(1024)(128)(2,1)}, u32[]{:S(2)}) copy-start(bf16[1408]{0:T(1024)(128)(2,1)} %param.16) | copy-start | bytes 8452
  6.5 25.6 %copy-start.3 = (bf16[2,88,2048]{2,1,0:T(8,128)(2,1)S(1)}, bf16[2,88,2048]{2,1,0:T(8,128)(2,1)}, u32[]{:S(2)}) copy-start(bf16[2,88,2048]{2,1,0:T(8,128)(2,1)} %param.19) | copy-start | bytes 2162692
  6.5 26.4 %copy-start.4 = (s32[2048]{0:T(1024)S(1)}, s32[2048]{0:T(1024)}, u32[]{:S(2)}) copy-start(s32[2048]{0:T(1024)} %param.21) | copy-start | bytes 24580
  6.5 83.5 %all-gather.3.cloned.1.call-start = ((), (), s32[]{:S(2)}) async-start(), calls=%async_computation.2 | async-start | bytes 6127616 | tf_op jit(solution)/shard_map/all_gather | solution.py:246
  11.8 20.1 %all-to-all-start = ((bf16[16,88,200]{2,1,0:T(8,128)(2,1)}), bf16[16,88,200]{2,1,0:T(8,128)(2,1)S(1)}, u32[]{:S(2)}, u32[]{:S(2)}) async-start(bf16[16,88,200]{2,1,0:T(8,128)(2,1)} %broadcast_in_dim.54), calls=%async_computation | async-start | bytes 1441792 | tf_op jit(solution)/shard_map/all_to_all | solution.py:250
  19.1 141.9 %all-gather.5.cloned.1.call-start = ((), (), s32[]{:S(2)}) async-start(), calls=%async_computation.3 | async-start | bytes 11489280 | tf_op jit(solution)/shard_map/all_gather | solution.py:290
  49.2 0.9 copy-start.2
  50.2 44.4 %copy-start.8 = (bf16[88,1408]{1,0:T(8,128)(2,1)S(1)}, bf16[88,1408]{1,0:T(8,128)(2,1)}, u32[]{:S(2)}) copy-start(bf16[88,1408]{1,0:T(8,128)(2,1)} %param.17) | copy-start | bytes 743428
  90.1 4.5 %copy-start.1 = (bf16[1408,2048]{1,0:T(8,128)(2,1)S(1)}, bf16[1408,2048]{1,0:T(8,128)(2,1)}, u32[]{:S(2)}) copy-start(bf16[1408,2048]{1,0:T(8,128)(2,1)} %all-gather.3.cloned.1.call-done) | copy-start | bytes 17301508
  108.0 75.6 %copy-start.6 = (bf16[1408]{0:T(1024)(128)(2,1)S(1)}, bf16[1408]{0:T(1024)(128)(2,1)}, u32[]{:S(2)}) copy-start(bf16[1408]{0:T(1024)(128)(2,1)} %param.23) | copy-start | bytes 8452
  161.0 31.4 %collective-permute-start = (bf16[5,1408,768]{2,1,0:T(8,128)(2,1)}, bf16[5,1408,768]{2,1,0:T(8,128)(2,1)}, u32[]{:S(2)}, u32[]{:S(2)}) collective-permute-start(bf16[5,1408,768]{2,1,0:T(8,128)(2,1)} %all-gather.5.cloned.1.call-done), channel_id=1, source_target_pairs={{0,16},{16,0},{32,48},{48,32},{64,80},{80,64},{96,112},{112,96},{1... | collective-permute-start | bytes 32440328 | tf_op jit(solution)/shard_map/ppermute | solution.py:304
  174.1 15.9 %all-to-all-start.1 = ((bf16[88,16,128]{2,0,1:T(8,128)(2,1)}), bf16[88,16,128]{2,0,1:T(8,128)(2,1)S(1)}, u32[]{:S(2)}, u32[]{:S(2)}) async-start(bf16[88,16,128]{2,0,1:T(8,128)(2,1)} %copy.70), calls=%async_computation.1 | async-start | bytes 720896 | tf_op jit(solution)/shard_map/all_to_all | solution.py:306
Sparse Core Ops, SparseCore 0:
  9.5 63.5 all-gather.2
  75.3 81.5 all-gather.4
where the time goes:
time: 243 us; the launch traced here: 242 us
  Pallas kernels  117 us (48%)
  starting transfers between devices  28 us (12%)
  local copies, waits for them, and re-layouts  24.9 us (10%)
  other arithmetic  24 us (10%)
  matrix products  17.2 us (7%)
  waiting for transfers between devices  16.3 us (7%)
  between operations  15.1 us (6%)
    pallas_call x1, Pallas kernels, attention(): pl.pallas_call(kernel, grid_spec=grid_spec, out_shape=jax.ShapeDtypeStruc...  53 us
    pallas_call x1, Pallas kernels, row_gather(): pl.pallas_call(functools.partial(_row_gather_kernel, n_row=n_row), out_sh...  39.9 us
    pallas_call x1, Pallas kernels, col_gather(): pl.pallas_call(functools.partial(_col_gather_kernel, n_col=n_col), out_sh...  24 us
    ppermute x1, starting transfers between devices, on_device(): lax.ppermute(weights_mine, 'row', [(i, i ^ 1) for i in range(n_row)])  11.1 us
    all_to_all x1, waiting for transfers between devices, on_device(): picked_full = lax.all_to_all(picked_copies, 'col', 0, 0, tiled=True)  10.6 us
    dot_general x2, matrix products, on_device(): jnp.einsum('fgi,ifd->gd', grouped, part[1:], preferred_element_type=jnp.f...  9.98 us
    all_to_all x1, starting transfers between devices, on_device(): attended_chunk = lax.all_to_all(attended, 'col', 1, 0, tiled=True)  9.47 us
    scatter x2, local copies, waits for them, and re-layouts, on_device(): keys_values = kv_cache.at[:, :, picked_rows].set(fresh_pairs)  7.64 us
  transfers between devices with their start and end apart: 5, of which 2 were waited for; matrix products, arithmetic and copies ran while one was open for 19% of the time, Pallas kernels for 38%

commit v1 on v0

--- a/solution.py
+++ b/solution.py
@@ -12,7 +12,7 @@
 EPSILON = 1e-06
 MASKED = -1e30
 PADW = 96
-Q_BLOCK = 2048
+Q_BLOCK = 512
 K_BLOCK = 2048
 
 

time: 243 us -> 238 us (0.979)
  starting transfers between devices: 28 us -> 16.2 us
  Pallas kernels: 117 us -> 126 us
  other arithmetic: 24 us -> 20.7 us
    ppermute x1, starting transfers between devices: 11.1 us -> 0.01 us  [on_device(): lax.ppermute(weights_mine, 'row', [(i, i ^ 1) for i in range(n_row)])]
    pallas_call x1, Pallas kernels: 53 us -> 60.6 us  [attention(): pl.pallas_call(kernel, grid_spec=grid_spec, out_shape=jax.ShapeDtypeStruc...]
  transfers between devices with their start and end apart: 5 -> 5, of which waited for: 2 -> 2; matrix products, arithmetic and copies ran while one was open for 19% -> 19% of each run, Pallas kernels for 38% -> 42%
where the time goes in v1:
time: 238 us; the launch traced here: 237 us
  Pallas kernels  126 us (53%)
  local copies, waits for them, and re-layouts  26.7 us (11%)
  other arithmetic  20.7 us (9%)
  matrix products  17.3 us (7%)
  waiting for transfers between devices  16.9 us (7%)
  starting transfers between devices  16.2 us (7%)
  between operations  13.7 us (6%)
    pallas_call x1, Pallas kernels, attention(): pl.pallas_call(kernel, grid_spec=grid_spec, out_shape=jax.ShapeDtypeStruc...  60.6 us
    pallas_call x1, Pallas kernels, row_gather(): pl.pallas_call(functools.partial(_row_gather_kernel, n_row=n_row), out_sh...  39.8 us
    pallas_call x1, Pallas kernels, col_gather(): pl.pallas_call(functools.partial(_col_gather_kernel, n_col=n_col), out_sh...  25.3 us
    all_to_all x1, waiting for transfers between devices, on_device(): picked_full = lax.all_to_all(picked_copies, 'col', 0, 0, tiled=True)  10.7 us
    dot_general x2, matrix products, on_device(): jnp.einsum('fgi,ifd->gd', grouped, part[1:], preferred_element_type=jnp.f...  9.98 us
    all_to_all x1, starting transfers between devices, on_device(): attended_chunk = lax.all_to_all(attended, 'col', 1, 0, tiled=True)  8.8 us
    scatter x2, local copies, waits for them, and re-layouts, on_device(): keys_values = kv_cache.at[:, :, picked_rows].set(fresh_pairs)  7.64 us
    all_to_all x1, starting transfers between devices, on_device(): picked_full = lax.all_to_all(picked_copies, 'col', 0, 0, tiled=True)  7.31 us
  transfers between devices with their start and end apart: 5, of which 2 were waited for; matrix products, arithmetic and copies ran while one was open for 19% of the time, Pallas kernels for 42%

profile of v1, /device:TPU:78, one launch (start us, length us, event | category | flops | bytes accessed | tf_op | source)
XLA Modules:
  0.0 237.3 jit_solution(3271596300253119431)
XLA Ops:
  6.6 0.7 all-gather.3.cloned.1.call-update
  7.3 1.3 copy.57
  8.5 0.7 compare_select_fusion
  9.2 0.8 gather_fusion
  10.0 0.7 compare_and_fusion.2
  10.9 0.9 broadcast_in_dim.60
  11.8 7.3 %all-to-all-start = ((bf16[16,88,200]{2,1,0:T(8,128)(2,1)}), bf16[16,88,200]{2,1,0:T(8,128)(2,1)S(1)}, u32[]{:S(2)}, u32[]{:S(2)}) async-start(bf16[16,88,200]{2,1,0:T(8,128)(2,1)} %broadcast_in_dim.60), calls=%async_computation | async-start | bytes 1441792 | tf_op jit(solution)/shard_map/all_to_all | solution.py:250
  19.2 2.2 fusion.31
  21.4 10.7 %all-to-all-done = bf16[16,88,200]{2,1,0:T(8,128)(2,1)S(1)} async-done(((bf16[16,88,200]{2,1,0:T(8,128)(2,1)}), bf16[16,88,200]{2,1,0:T(8,128)(2,1)S(1)}, u32[]{:S(2)}, u32[]{:S(2)}) %all-to-all-start) | async-done | bytes 563232 | tf_op jit(solution)/shard_map/all_to_all | solution.py:250
  32.2 0.8 copy.60
  33.2 1.4 copy.71.qs_ref
  34.8 0.7 fusion.42
  35.5 0.7 and_reduce_fusion
  36.8 0.3 convolution_convert_fusion
  37.2 6.9 %scatter_fusion = bf16[2,88,2048]{1,0,2:T(2,128)(2,1)S(1)} fusion(bf16[2,88,2048]{1,0,2:T(2,128)(2,1)S(1)} %copy.60, s32[200]{0:T(256)S(1)} %bitcast.84, bf16[200,2,88]{2,1,0:T(2,128)(2,1)S(1)} %bitcast.76), kind=kCustom, calls=%fused_computation.7 | custom fusion | bytes 212000 | tf_op jit(solution)/shard_map/scatter | solution.py:265
  44.1 0.8 copy.61
  45.0 1.9 broadcast_select_fusion
  46.9 1.6 scatter.13.x_ref
  48.5 0.9 copy-done.2
  49.4 39.8 %shard_map.109.k_ref.v_ref = bf16[8,2,96,2048]{3,2,1,0:T(8,128)(2,1)} custom-call(bf16[2,96,2048]{2,1,0:T(8,128)(2,1)} %copy-done.2), custom_call_target="tpu_custom_call" | custom-call | tf_op jit(solution)/shard_map/pallas_call | solution.py:110
  89.2 4.4 %convert_reduce_fusion = (f32[2048]{0:T(1024)S(1)}, f32[2048]{0:T(1024)S(1)}) fusion(bf16[1408,2048]{1,0:T(8,128)(2,1)} %all-gather.3.cloned.1.call-done), kind=kLoop, calls=%fused_computation.10 | loop fusion | flops 11530240 | bytes 5783552 | tf_op jit(solution)/shard_map/reduce_sum | solution.py:272
  93.7 2.0 fusion.10
  96.0 0.9 pad.17.q_ref
  96.9 1.0 slice_convert_fusion
  98.4 0.8 gather_fusion.4
  99.3 0.7 gather_fusion.5
  100.7 0.7 sort.17
  101.5 0.8 gather_fusion.2
  102.4 0.7 gather_fusion.6
  103.3 0.6 select_select_fusion
  103.9 0.6 gather_fusion.3
  104.6 0.7 fusion.37.kb_map
  105.2 60.6 %shard_map.110 = bf16[2048,96]{1,0:T(8,128)(2,1)} custom-call(s32[4,8]{1,0:T(4,128)} %fusion.37.kb_map, s32[4,8]{1,0:T(4,128)} %get-tuple-element.38.flags, bf16[2048,96]{1,0:T(8,128)(2,1)} %pad.17.q_ref, f32[2048,1]{1,0:T(8,128)} %copy.71.qs_ref, bf16[8,2,96,2048]{3,2,1,0:T(8,128)(2,1)} %shard_map.109.k_ref.v_ref, ...), custom_call_target="tpu_custom_call" | custom-call | tf_op jit(solution)/shard_map/pallas_call | solution.py:217
  165.8 2.0 copy.72
  167.8 8.8 %all-to-all-start.1 = ((bf16[88,16,128]{2,0,1:T(8,128)(2,1)}), bf16[88,16,128]{2,0,1:T(8,128)(2,1)S(1)}, u32[]{:S(2)}, u32[]{:S(2)}) async-start(bf16[88,16,128]{2,0,1:T(8,128)(2,1)} %copy.72), calls=%async_computation.1 | async-start | bytes 720896 | tf_op jit(solution)/shard_map/all_to_all | solution.py:306
  176.6 0.7 fusion.38
  177.3 0.7 compare_bitcast_fusion
  178.0 5.5 %all-to-all-done.1 = bf16[88,16,128]{2,0,1:T(8,128)(2,1)S(1)} async-done(((bf16[88,16,128]{2,0,1:T(8,128)(2,1)}), bf16[88,16,128]{2,0,1:T(8,128)(2,1)S(1)}, u32[]{:S(2)}, u32[]{:S(2)}) %all-to-all-start.1) | async-done | bytes 360480 | tf_op jit(solution)/shard_map/all_to_all | solution.py:306
  183.6 2.4 %fusion.14 = f32[768,128]{1,0:T(8,128)S(1)} fusion(bf16[1408,128]{1,0:T(8,128)(2,1)S(1)} %bitcast.77, bf16[5,1408,768]{2,1,0:T(8,128)(2,1)} %all-gather.5.cloned.1.call-done), kind=kOutput, calls=%fused_computation.23 | convolution fusion | flops 276824064 | bytes 2916352 | tf_op jit(solution)/shard_map/dot_general | solution.py:310
  185.9 2.4 %fusion.13 = f32[768,128]{1,0:T(8,128)S(1)} fusion(bf16[1408,128]{1,0:T(8,128)(2,1)S(1)} %bitcast.78, bf16[5,1408,768]{2,1,0:T(8,128)(2,1)} %collective-permute-done), kind=kOutput, calls=%fused_computation.22 | convolution fusion | flops 276824064 | bytes 2916352 | tf_op jit(solution)/shard_map/dot_general | solution.py:310
  188.3 1.2 fusion.40
  189.5 1.2 multiply_convert_fusion
  191.1 5.0 %fusion.23 = bf16[32,768]{1,0:T(8,128)(2,1)S(1)} fusion(bf16[5,1408,768]{2,1,0:T(8,128)(2,1)} %all-gather.5.cloned.1.call-done, bf16[1408,32,4]{0,2,1:T(4,128)(2,1)S(1)} %reshape.357), kind=kOutput, calls=%fused_computation.39 | convolution fusion | flops 276824064 | bytes 9060352 | tf_op jit(solution)/shard_map/fgi,ifd->gd/dot_general | solution.py:328
  196.1 5.0 %fusion.26 = bf16[32,768]{1,0:T(8,128)(2,1)S(1)} fusion(bf16[5,1408,768]{2,1,0:T(8,128)(2,1)} %collective-permute-done, bf16[1408,32,4]{0,2,1:T(4,128)(2,1)S(1)} %reshape.357), kind=kOutput, calls=%fused_computation.40 | convolution fusion | flops 276824064 | bytes 9060352 | tf_op jit(solution)/shard_map/fgi,ifd->gd/dot_general | solution.py:328
  201.1 0.7 fusion.35.x_ref
  201.8 25.3 %shard_map.111 = bf16[16,32,1408]{2,1,0:T(8,128)(2,1)} custom-call(bf16[32,1408]{1,0:T(8,128)(2,1)} %fusion.35.x_ref), custom_call_target="tpu_custom_call" | custom-call | tf_op jit(solution)/shard_map/pallas_call | solution.py:154
  227.1 2.5 %gather_fusion.1 = bf16[85,1408]{1,0:T(8,128)(2,1)S(1)} fusion(bf16[512,1408]{1,0:T(8,128)(2,1)} %bitcast.73, s32[1024]{0:T(1024)S(1)} %pad_clamp_fusion), kind=kCustom, calls=%fused_computation.4 | custom fusion | bytes 479060 | tf_op jit(solution)/shard_map/gather | solution.py:337
  229.6 0.8 bitcast_select_fusion
  (75 shorter events, 3.9 us)
Async XLA Ops:
  6.5 30.2 %copy-start = (bf16[2,88,1408]{2,1,0:T(8,128)(2,1)S(1)}, bf16[2,88,1408]{2,1,0:T(8,128)(2,1)}, u32[]{:S(2)}) copy-start(bf16[2,88,1408]{2,1,0:T(8,128)(2,1)} %param.18) | copy-start | bytes 1486852
  6.5 29.0 %copy-start.7 = (s32[3]{0:T(128)S(1)}, s32[3]{0:T(128)}, u32[]{:S(2)}) copy-start(s32[3]{0:T(128)} %constant.169.clone.1) | copy-start | bytes 40
  6.5 25.6 %copy-start.5 = (bf16[1408]{0:T(1024)(128)(2,1)S(1)}, bf16[1408]{0:T(1024)(128)(2,1)}, u32[]{:S(2)}) copy-start(bf16[1408]{0:T(1024)(128)(2,1)} %param.16) | copy-start | bytes 8452
  6.5 25.7 %copy-start.3 = (bf16[2,88,2048]{2,1,0:T(8,128)(2,1)S(1)}, bf16[2,88,2048]{2,1,0:T(8,128)(2,1)}, u32[]{:S(2)}) copy-start(bf16[2,88,2048]{2,1,0:T(8,128)(2,1)} %param.19) | copy-start | bytes 2162692
  6.5 26.5 %copy-start.4 = (s32[2048]{0:T(1024)S(1)}, s32[2048]{0:T(1024)}, u32[]{:S(2)}) copy-start(s32[2048]{0:T(1024)} %param.21) | copy-start | bytes 24580
  6.5 82.6 %all-gather.3.cloned.1.call-start = ((), (), s32[]{:S(2)}) async-start(), calls=%async_computation.2 | async-start | bytes 6127616 | tf_op jit(solution)/shard_map/all_gather | solution.py:246
  11.8 20.3 %all-to-all-start = ((bf16[16,88,200]{2,1,0:T(8,128)(2,1)}), bf16[16,88,200]{2,1,0:T(8,128)(2,1)S(1)}, u32[]{:S(2)}, u32[]{:S(2)}) async-start(bf16[16,88,200]{2,1,0:T(8,128)(2,1)} %broadcast_in_dim.60), calls=%async_computation | async-start | bytes 1441792 | tf_op jit(solution)/shard_map/all_to_all | solution.py:250
  19.1 146.7 %all-gather.5.cloned.1.call-start = ((), (), s32[]{:S(2)}) async-start(), calls=%async_computation.3 | async-start | bytes 11489280 | tf_op jit(solution)/shard_map/all_gather | solution.py:290
  48.5 0.9 copy-start.2
  49.4 44.2 %copy-start.8 = (bf16[88,1408]{1,0:T(8,128)(2,1)S(1)}, bf16[88,1408]{1,0:T(8,128)(2,1)}, u32[]{:S(2)}) copy-start(bf16[88,1408]{1,0:T(8,128)(2,1)} %param.17) | copy-start | bytes 743428
  89.2 4.5 %copy-start.1 = (bf16[1408,2048]{1,0:T(8,128)(2,1)S(1)}, bf16[1408,2048]{1,0:T(8,128)(2,1)}, u32[]{:S(2)}) copy-start(bf16[1408,2048]{1,0:T(8,128)(2,1)} %all-gather.3.cloned.1.call-done) | copy-start | bytes 17301508
  105.2 71.4 %copy-start.6 = (bf16[1408]{0:T(1024)(128)(2,1)S(1)}, bf16[1408]{0:T(1024)(128)(2,1)}, u32[]{:S(2)}) copy-start(bf16[1408]{0:T(1024)(128)(2,1)} %param.23) | copy-start | bytes 8452
  165.8 20.1 %collective-permute-start = (bf16[5,1408,768]{2,1,0:T(8,128)(2,1)}, bf16[5,1408,768]{2,1,0:T(8,128)(2,1)}, u32[]{:S(2)}, u32[]{:S(2)}) collective-permute-start(bf16[5,1408,768]{2,1,0:T(8,128)(2,1)} %all-gather.5.cloned.1.call-done), channel_id=1, source_target_pairs={{0,16},{16,0},{32,48},{48,32},{64,80},{80,64},{96,112},{112,96},{1... | collective-permute-start | bytes 32440328 | tf_op jit(solution)/shard_map/ppermute | solution.py:304
  167.8 15.7 %all-to-all-start.1 = ((bf16[88,16,128]{2,0,1:T(8,128)(2,1)}), bf16[88,16,128]{2,0,1:T(8,128)(2,1)S(1)}, u32[]{:S(2)}, u32[]{:S(2)}) async-start(bf16[88,16,128]{2,0,1:T(8,128)(2,1)} %copy.72), calls=%async_computation.1 | async-start | bytes 720896 | tf_op jit(solution)/shard_map/all_to_all | solution.py:306
Sparse Core Ops, SparseCore 0:
  9.5 63.5 all-gather.2
  75.3 81.5 all-gather.4
